TPU v7x, 32 devices: a whole 2x2x4 slice. The times are simulated.
32 devices in a mesh: grp: 2 (over y), tile: 4 (over z), span: 4 (over x, core).
Axes of the slice: x: 2, y: 2, z: 4, core: 2. Of those that a mesh axis runs over, the one named last changes fastest.
Arguments:
- features: bfloat16 [16, 8, 160, 384], P(('grp', 'span'), 'tile'), parts along dimension 0, may hold values from -24 to 24
- clip_lengths: int32 [8], P('grp'), parts along dimension 0, may hold values from 1 to 4, as said below
- norm_gain: float32 [384], replicated, may hold values from 0.1 to 1.9
- w_qkv: bfloat16 [384, 1152], replicated, may hold values from -6 to 6
- w_out: bfloat16 [384, 384], replicated, may hold values from -1 to 1
- conv_gain: float32 [384], replicated, may hold values from 0.1 to 1.9
- w_conv: bfloat16 [3, 3, 3, 384, 384], replicated, may hold values from -0.0625 to 0.0625
Outputs:
- attended: bfloat16 [16, 8, 160, 384], P(('grp', 'span'), 'tile'), parts along dimension 0
- hidden: bfloat16 [16, 8, 160, 384], P(('grp', 'span'), 'tile'), parts along dimension 0
There are 2 independent parts, one for each index of `grp`. A program takes and returns all parts, laid end to end along the dimension named above; an argument that names none is the same for every part. Nothing has to cross between parts.
Inputs may be any that keep to these rules, and one draw needn't show every extreme that they name: `clip_lengths`: the lengths sum to 8; exactly one clip has 4 frames.
All inputs are finite; a program needn't handle non-finite values.
Results may differ from a plain program's by a relative error of at most 0.0095.
The roundings to bfloat16 on the way count: a program that leaves them out, or rounds other values in their place, can miss the bound.
Values may be sent and summed in bfloat16 or wider, within the bound.
No kernel may reach another device: no remote copies, remote signals or barrier semaphores. Data moves between devices by JAX's collectives and lax.ppermute only.
A program may use at most 128 MiB of HBM per device.

v0:
```python
import jax
import jax.numpy as jnp
from jax import lax
from jax.sharding import PartitionSpec as P

eps = 1e-06


def from_behind(block, axis, distance):
    devices = range(lax.axis_size(axis))
    route = [(i - distance, i) for i in devices if i - distance in devices]
    return lax.ppermute(block, axis, route)


def extended(x, sides, width):
    for axis, dim in sides:
        size, length = (lax.axis_size(axis), x.shape[dim])
        up = [(i, (i + 1) % size) for i in range(size - 1)]
        down = [(j, i) for i, j in up]
        last = lax.slice_in_dim(x, length - width, length, axis=dim)
        first = lax.slice_in_dim(x, 0, width, axis=dim)
        before = lax.ppermute(last, axis, up)
        after = lax.ppermute(first, axis, down)
        x = jnp.concatenate([before, x, after], axis=dim)
    return x


def rms_scale(values, gain_vec):
    as_float = values.astype(jnp.float32)
    return (
        as_float * lax.rsqrt(jnp.mean(as_float * as_float, axis=-1, keepdims=True) + eps) * gain_vec
    )


def on_device(features, clip_lengths, norm_gain, w_qkv, w_out, conv_gain, w_conv):
    frames, row_count, col_count, channels = features.shape
    cell_count = row_count * col_count
    normed_grid = rms_scale(features, norm_gain).astype(jnp.bfloat16)
    view_frames = normed_grid.shape[0]
    view_cells = normed_grid.shape[1] * normed_grid.shape[2]
    normed = normed_grid.reshape(view_frames, view_cells, channels)
    queries = jnp.dot(
        normed.reshape(-1, channels), w_qkv[:, :channels], preferred_element_type=jnp.float32
    )
    queries = queries.astype(jnp.bfloat16).reshape(view_frames, view_cells, channels)
    kv_weight = w_qkv[:, channels:]
    score_scale = channels ** (-0.5)
    outgoing = jnp.dot(normed.reshape(-1, channels), kv_weight, preferred_element_type=jnp.float32)
    outgoing = outgoing.astype(jnp.bfloat16).reshape(view_frames, view_cells, 2 * channels)
    portion = lax.all_gather(outgoing, "tile", axis=1, tiled=True)
    key_part = portion[:, :, :channels]
    value_part = portion[:, :, channels:]
    row_top = jnp.full((view_frames, view_cells, 1), -1e30, jnp.float32)
    scores = (
        jnp.einsum("fqc,fkc->fqk", queries, key_part, preferred_element_type=jnp.float32)
        * score_scale
    )
    new_top = jnp.maximum(row_top, jnp.max(scores, axis=2, keepdims=True))
    raised_f = jnp.exp(scores - new_top)
    row_total = jnp.sum(raised_f, axis=2, keepdims=True)
    weighted = jnp.einsum(
        "fqk,fkc->fqc",
        raised_f.astype(jnp.bfloat16),
        value_part,
        preferred_element_type=jnp.float32,
    )
    mixture_grid = (weighted / row_total).astype(jnp.bfloat16)
    mixture = mixture_grid.reshape(-1, channels)
    projected = jnp.dot(mixture, w_out, preferred_element_type=jnp.float32)
    attended = (features.reshape(-1, channels).astype(jnp.float32) + projected).astype(jnp.bfloat16)
    attended = attended.reshape(frames, row_count, col_count, channels)
    lifted = rms_scale(attended, conv_gain)
    activated = (lifted * jax.nn.sigmoid(lifted)).astype(jnp.bfloat16)
    earlier = from_behind(activated, "span", 1)
    stacked = jnp.concatenate([earlier, activated], axis=0)
    edged = extended(stacked, (("tile", 1),), 1)
    padded = jnp.pad(edged, ((0, 0), (0, 0), (1, 1), (0, 0)))
    clip_ends = jnp.cumsum(clip_lengths)
    position = lax.axis_index("span") * frames + jnp.arange(frames, dtype=jnp.int32)
    clip_start = jnp.sum(
        jnp.where(clip_ends[None, :] <= position[:, None], clip_lengths[None, :], 0), axis=1
    )
    summed = jnp.zeros((frames * cell_count, channels), jnp.float32)
    for t_tap in range(3):
        usable = position - (2 - t_tap) >= clip_start
        for r_tap in range(3):
            for c_tap in range(3):
                shifted = padded[
                    t_tap : t_tap + frames, r_tap : r_tap + row_count, c_tap : c_tap + col_count
                ]
                shifted = jnp.where(
                    usable[:, None, None, None], shifted, jnp.zeros((), shifted.dtype)
                )
                summed = summed + jnp.dot(
                    shifted.reshape(-1, channels),
                    w_conv[t_tap, r_tap, c_tap],
                    preferred_element_type=jnp.float32,
                )
    hidden = summed.astype(jnp.bfloat16).reshape(frames, row_count, col_count, channels)
    return (attended, hidden)


def solution(mesh):
    in_specs = (P(("grp", "span"), "tile", None, None), P("grp"), P(), P(), P(), P(), P())
    out_specs = (P(("grp", "span"), "tile", None, None), P(("grp", "span"), "tile", None, None))
    return jax.shard_map(
        on_device, mesh=mesh, in_specs=in_specs, out_specs=out_specs, check_vma=False
    )
```

profile of v0, /device:TPU:10, one launch (start us, length us, event | category | flops | bytes accessed | tf_op | source)
XLA Modules:
  0.0 146.0 jit_solution(7980055820085720016)
XLA Ops:
  7.2 1.3 multiply_reduce_fusion
  8.5 1.2 multiply_convert_fusion.1
  9.8 2.7 %convolution_convert_fusion = bf16[640,768]{1,0:T(8,128)(2,1)} fusion(bf16[640,384]{1,0:T(8,128)(2,1)S(1)} %bitcast.177, bf16[384,1152]{1,0:T(8,128)(2,1)} %param.10), kind=kOutput, calls=%fused_computation.18 | convolution fusion | flops 377978880 | bytes 2064384 | tf_op jit(solution)/shard_map/dot_general | solution.py:48
  12.5 1.4 convolution_convert_fusion.1
  13.9 73.9 %all-gather.2.cloned.1.call-done = bf16[2,1280,768]{2,1,0:T(8,128)(2,1)} async-done(((bf16[2,320,768]{2,1,0:T(8,128)(2,1)}), bf16[2,1280,768]{2,1,0:T(8,128)(2,1)}) %all-gather.2.cloned.1.call-update) | async-done | bytes 3932176 | tf_op jit(solution)/shard_map/all_gather | solution.py:50
  87.8 2.8 %fusion.98 = (f32[2,320]{1,0:T(2,128)S(1)}, f32[2,320,1280]{2,1,0:T(8,128)S(1)}) fusion(bf16[2,320,384]{2,1,0:T(8,128)(2,1)S(1)} %bitcast.179, bf16[2,1280,768]{2,1,0:T(8,128)(2,1)} %all-gather.2.cloned.1.call-done), kind=kOutput, calls=%fused_computation.171 | convolution fusion | flops 630783360 | bytes 5736960 | tf_op jit(solution)/shard_map/fqc,fkc->fqk/dot_general | solution.py:55
  90.6 0.6 fusion.1
  91.3 1.1 divide_convert_fusion
  92.4 0.6 fusion.14
  93.5 1.9 %collective-permute-start = (bf16[2,2,160,384]{3,2,1,0:T(8,128)(2,1)S(1)}, bf16[2,2,160,384]{3,2,1,0:T(8,128)(2,1)S(1)}, u32[]{:S(2)}, u32[]{:S(2)}) collective-permute-start(bf16[2,2,160,384]{3,2,1,0:T(8,128)(2,1)S(1)} %multiply_convert_fusion), channel_id=1, source_target_pairs={{0,1},{1,2},{2,3},{4,5},{5,6},{6,7},{8,9},{9,10},{10,11},{12,13},{... | collective-permute-start | bytes 1474568 | tf_op jit(solution)/shard_map/ppermute | solution.py:12
  95.4 8.2 %collective-permute-done = bf16[2,2,160,384]{3,2,1,0:T(8,128)(2,1)S(1)} collective-permute-done((bf16[2,2,160,384]{3,2,1,0:T(8,128)(2,1)S(1)}, bf16[2,2,160,384]{3,2,1,0:T(8,128)(2,1)S(1)}, u32[]{:S(2)}, u32[]{:S(2)}) %collective-permute-start) | collective-permute-done | bytes 491552 | tf_op jit(solution)/shard_map/ppermute | solution.py:12
  103.6 0.9 fusion.30
  104.5 4.4 %collective-permute-start.1 = (bf16[4,1,160,384]{3,2,1,0:T(8,128)(2,1)}, bf16[4,1,160,384]{3,2,1,0:T(8,128)(2,1)S(1)}, u32[]{:S(2)}, u32[]{:S(2)}) collective-permute-start(bf16[4,1,160,384]{3,2,1,0:T(8,128)(2,1)} %get-tuple-element.34), channel_id=1, source_target_pairs={{0,4},{4,8},{8,12},{1,5},{5,9},{9,13},{2,6},{6,10},{10,14},{3,7},{... | collective-permute-start | bytes 1474568 | tf_op jit(solution)/shard_map/ppermute | solution.py:22
  108.9 1.9 %collective-permute-start.2 = (bf16[4,1,160,384]{3,2,1,0:T(8,128)(2,1)S(1)}, bf16[4,1,160,384]{3,2,1,0:T(8,128)(2,1)S(1)}, u32[]{:S(2)}, u32[]{:S(2)}) collective-permute-start(bf16[4,1,160,384]{3,2,1,0:T(8,128)(2,1)S(1)} %get-tuple-element.35), channel_id=1, source_target_pairs={{4,0},{8,4},{12,8},{5,1},{9,5},{13,9},{6,2},{10,6},{14,10},{7,3},{... | collective-permute-start | bytes 1474568 | tf_op jit(solution)/shard_map/ppermute | solution.py:23
  111.4 4.4 %collective-permute-done.1 = bf16[4,1,160,384]{3,2,1,0:T(8,128)(2,1)S(1)} collective-permute-done((bf16[4,1,160,384]{3,2,1,0:T(8,128)(2,1)}, bf16[4,1,160,384]{3,2,1,0:T(8,128)(2,1)S(1)}, u32[]{:S(2)}, u32[]{:S(2)}) %collective-permute-start.1) | collective-permute-done | bytes 491552 | tf_op jit(solution)/shard_map/ppermute | solution.py:22
  115.8 3.9 %collective-permute-done.2 = bf16[4,1,160,384]{3,2,1,0:T(8,128)(2,1)S(1)} collective-permute-done((bf16[4,1,160,384]{3,2,1,0:T(8,128)(2,1)S(1)}, bf16[4,1,160,384]{3,2,1,0:T(8,128)(2,1)S(1)}, u32[]{:S(2)}, u32[]{:S(2)}) %collective-permute-start.2) | collective-permute-done | bytes 491552 | tf_op jit(solution)/shard_map/ppermute | solution.py:23
  119.6 1.2 select_maximum_fusion
  120.8 1.4 slice_select_fusion
  122.5 1.5 %slice_select_fusion.6 = (bf16[2,2,160,384]{3,2,1,0:T(8,128)(2,1)S(1)}, bf16[2,2,160,384]{3,2,1,0:T(8,128)(2,1)S(1)}, bf16[2,2,160,384]{3,2,1,0:T(8,128)(2,1)S(1...) fusion(bf16[4,3,160,384]{3,2,1,0:T(8,128)(2,1)S(1)} %get-tuple-, ...), kind=kLoop, calls=%fused_computation.77 | loop fusion | flops 3686400 | bytes 13762566 | tf_op jit(solution)/shard_map/jit(_where)/select_n | solution.py:91
  124.3 1.3 slice-done.1
  127.0 0.5 convolution_add_fusion.23
  128.4 0.5 convolution_add_fusion.20
  135.8 0.6 convolution_add_fusion.4
  137.9 1.2 fusion.13
  (53 shorter events, 12.0 us)
Async XLA Ops:
  7.2 85.3 %copy-start = (bf16[384,384]{1,0:T(8,128)(2,1)S(1)}, bf16[384,384]{1,0:T(8,128)(2,1)}, u32[]{:S(2)}) copy-start(bf16[384,384]{1,0:T(8,128)(2,1)} %param.11) | copy-start | bytes 884740
  7.2 80.6 %all-gather.2.cloned.1.call-start = ((), (), s32[]{:S(2)}) async-start(), calls=%async_computation | async-start | bytes 4915200 | tf_op jit(solution)/shard_map/all_gather | solution.py:50
  87.8 3.5 %copy-start.2 = (bf16[2,1280,768]{2,1,0:T(8,128)(2,1)S(1)}, bf16[2,1280,768]{2,1,0:T(8,128)(2,1)}, u32[]{:S(2)}) copy-start(bf16[2,1280,768]{2,1,0:T(8,128)(2,1)} %all-gather.2.cloned.1.call-done) | copy-start | bytes 11796484
  91.3 1.1 copy-start.1
  91.3 1.8 %copy-start.4 = (f32[384]{0:T(512)S(1)}, f32[384]{0:T(512)}, u32[]{:S(2)}) copy-start(f32[384]{0:T(512)} %param.12) | copy-start | bytes 4612
  92.4 18.4 %copy-start.5 = (s32[4]{0:T(128)S(1)}, s32[4]{0:T(128)}, u32[]{:S(2)}) copy-start(s32[4]{0:T(128)} %param.8) | copy-start | bytes 52
  93.0 42.8 %copy-start.3 = (bf16[640,384]{1,0:T(8,128)(2,1)}, bf16[640,384]{1,0:T(8,128)(2,1)S(1)}, u32[]{:S(2)}) copy-start(bf16[640,384]{1,0:T(8,128)(2,1)S(1)} %get-tuple-element.55) | copy-start | bytes 1474564
  93.5 10.1 %collective-permute-start = (bf16[2,2,160,384]{3,2,1,0:T(8,128)(2,1)S(1)}, bf16[2,2,160,384]{3,2,1,0:T(8,128)(2,1)S(1)}, u32[]{:S(2)}, u32[]{:S(2)}) collective-permute-start(bf16[2,2,160,384]{3,2,1,0:T(8,128)(2,1)S(1)} %multiply_convert_fusion), channel_id=1, source_target_pairs={{0,1},{1,2},{2,3},{4,5},{5,6},{6,7},{8,9},{9,10},{10,11},{12,13},{... | collective-permute-start | bytes 1474568 | tf_op jit(solution)/shard_map/ppermute | solution.py:12
  104.5 11.2 %collective-permute-start.1 = (bf16[4,1,160,384]{3,2,1,0:T(8,128)(2,1)}, bf16[4,1,160,384]{3,2,1,0:T(8,128)(2,1)S(1)}, u32[]{:S(2)}, u32[]{:S(2)}) collective-permute-start(bf16[4,1,160,384]{3,2,1,0:T(8,128)(2,1)} %get-tuple-element.34), channel_id=1, source_target_pairs={{0,4},{4,8},{8,12},{1,5},{5,9},{9,13},{2,6},{6,10},{10,14},{3,7},{... | collective-permute-start | bytes 1474568 | tf_op jit(solution)/shard_map/ppermute | solution.py:22
  108.9 10.7 %collective-permute-start.2 = (bf16[4,1,160,384]{3,2,1,0:T(8,128)(2,1)S(1)}, bf16[4,1,160,384]{3,2,1,0:T(8,128)(2,1)S(1)}, u32[]{:S(2)}, u32[]{:S(2)}) collective-permute-start(bf16[4,1,160,384]{3,2,1,0:T(8,128)(2,1)S(1)} %get-tuple-element.35), channel_id=1, source_target_pairs={{4,0},{8,4},{12,8},{5,1},{9,5},{13,9},{6,2},{10,6},{14,10},{7,3},{... | collective-permute-start | bytes 1474568 | tf_op jit(solution)/shard_map/ppermute | solution.py:23
  122.2 2.1 %slice-start = ((s8[7962624]{0:T(1024)(128)(4,1)}), s8[3768320]{0:T(1024)(128)(4,1)S(1)}, s32[]{:S(2)}) async-start(s8[7962624]{0:T(1024)(128)(4,1)} %bitcast.148), calls=%async_computation.1 | async-start | bytes 7536640
  122.5 3.1 %slice-start.1 = ((s8[7962624]{0:T(1024)(128)(4,1)}), s8[4194304]{0:T(1024)(128)(4,1)S(1)}, s32[]{:S(2)}) async-start(s8[7962624]{0:T(1024)(128)(4,1)} %bitcast.148), calls=%async_computation.2 | async-start | bytes 8388608
Sparse Core Ops, SparseCore 0:
  12.6 75.1 all-gather.1
where the time goes:
time: 146 us
  waiting for transfers between devices  90.4 us (62%)
  matrix products  21.9 us (15%)
  between operations  14.4 us (10%)
  other arithmetic  9.18 us (6%)
  starting transfers between devices  8.25 us (6%)
  local copies, waits for them, and re-layouts  1.85 us (1%)
    all_gather x1, waiting for transfers between devices, on_device(): portion = lax.all_gather(outgoing, 'tile', axis=1, tiled=True)  73.9 us
    dot_general x27, matrix products, on_device(): jnp.dot(shifted.reshape(-1, channels), w_conv[t_tap, r_tap, c_tap], prefe...  13.3 us
    ppermute x1, waiting for transfers between devices, from_behind(): return lax.ppermute(block, axis, route)  8.22 us
    ppermute x1, starting transfers between devices, extended(): before = lax.ppermute(last, axis, up)  4.37 us
    ppermute x1, waiting for transfers between devices, extended(): before = lax.ppermute(last, axis, up)  4.36 us
    ppermute x1, waiting for transfers between devices, extended(): after = lax.ppermute(first, axis, down)  3.87 us
    select_n x2, other arithmetic, on_device(): jnp.where(usable[:, None, None, None], shifted, jnp.zeros((), shifted.dty...  2.92 us
  transfers between devices with their start and end apart: 4, of which 4 were waited for; matrix products, arithmetic and copies ran while one was open for 1% of the time, Pallas kernels for 0%

commit v1 on v0

--- a/solution.py
+++ b/solution.py
@@ -4,6 +4,24 @@
 from jax.sharding import PartitionSpec as P
 
 eps = 1e-06
+
+
+def ring_gather(shard, axis, dim):
+    ways, here, step = (lax.axis_size(axis), lax.axis_index(axis), shard.shape[dim])
+    shape = [n * ways if d == dim else n for d, n in enumerate(shard.shape)]
+    full = lax.dynamic_update_slice_in_dim(
+        jnp.zeros(shape, shard.dtype), shard, here * step, axis=dim
+    )
+    going_up = going_down = shard
+    for far in range(1, ways // 2 + 1):
+        going_up = lax.ppermute(going_up, axis, [(d, (d + 1) % ways) for d in range(ways)])
+        full = lax.dynamic_update_slice_in_dim(full, going_up, (here - far) % ways * step, axis=dim)
+        if 2 * far < ways:
+            going_down = lax.ppermute(going_down, axis, [(d, (d - 1) % ways) for d in range(ways)])
+            full = lax.dynamic_update_slice_in_dim(
+                full, going_down, (here + far) % ways * step, axis=dim
+            )
+    return full
 
 
 def from_behind(block, axis, distance):
@@ -47,7 +65,7 @@
     score_scale = channels ** (-0.5)
     outgoing = jnp.dot(normed.reshape(-1, channels), kv_weight, preferred_element_type=jnp.float32)
     outgoing = outgoing.astype(jnp.bfloat16).reshape(view_frames, view_cells, 2 * channels)
-    portion = lax.all_gather(outgoing, "tile", axis=1, tiled=True)
+    portion = ring_gather(outgoing, "tile", 1)
     key_part = portion[:, :, :channels]
     value_part = portion[:, :, channels:]
     row_top = jnp.full((view_frames, view_cells, 1), -1e30, jnp.float32)

time: 146 us -> 120 us (0.82)
  waiting for transfers between devices: 90.4 us -> 56.1 us
  starting transfers between devices: 8.25 us -> 30.3 us
  between operations: 14.4 us -> 1.09 us
  local copies, waits for them, and re-layouts: 1.85 us -> 4.79 us
  matrix products: 21.9 us -> 19.3 us
    all_gather x1 -> x0, waiting for transfers between devices: 73.9 us -> none  [on_device(): portion = lax.all_gather(outgoing, 'tile', axis=1, tiled=True)]
    ppermute x0 -> x3, waiting for transfers between devices: none -> 40.2 us  [the longest x2 40.2 us: ring_gather(): lax.ppermute(going_up, axis, [(d, (d + 1) % ways) for d in range(ways)])]
    ppermute x0 -> x3, starting transfers between devices: none -> 22.5 us  [the longest x2 22 us: ring_gather(): lax.ppermute(going_up, axis, [(d, (d + 1) % ways) for d in range(ways)])]
    dynamic_update_slice x0 -> x4, local copies, waits for them, and re-layouts: none -> 2.74 us  [the longest x2 1.36 us: ring_gather(): lax.dynamic_update_slice_in_dim(full, going_up, (here - far) % ways * ste...]
    dot_general x1, matrix products: 2.83 us -> 1.16 us  [on_device(): jnp.einsum('fqc,fkc->fqk', queries, key_part, preferred_element_type=jnp....]
  transfers between devices with their start and end apart: 4 -> 6, of which waited for: 4 -> 5; matrix products, arithmetic and copies ran while one was open for 1% -> 3% of each run, Pallas kernels for 0% -> 0%
where the time goes in v1:
time: 120 us
  waiting for transfers between devices  56.1 us (47%)
  starting transfers between devices  30.3 us (25%)
  matrix products  19.3 us (16%)
  other arithmetic  8.47 us (7%)
  local copies, waits for them, and re-layouts  4.79 us (4%)
    ppermute x2, waiting for transfers between devices, ring_gather(): lax.ppermute(going_up, axis, [(d, (d + 1) % ways) for d in range(ways)])  40.2 us
    ppermute x2, starting transfers between devices, ring_gather(): lax.ppermute(going_up, axis, [(d, (d + 1) % ways) for d in range(ways)])  22 us
    dot_general x27, matrix products, on_device(): jnp.dot(shifted.reshape(-1, channels), w_conv[t_tap, r_tap, c_tap], prefe...  13.3 us
    ppermute x1, waiting for transfers between devices, from_behind(): return lax.ppermute(block, axis, route)  8.22 us
    ppermute x1, waiting for transfers between devices, extended(): before = lax.ppermute(last, axis, up)  4.28 us
    ppermute x1, waiting for transfers between devices, extended(): after = lax.ppermute(first, axis, down)  3.45 us
    ppermute x1, starting transfers between devices, extended(): before = lax.ppermute(last, axis, up)  3.44 us
    select_n x2, other arithmetic, on_device(): jnp.where(usable[:, None, None, None], shifted, jnp.zeros((), shifted.dty...  2.98 us
  transfers between devices with their start and end apart: 6, of which 5 were waited for; matrix products, arithmetic and copies ran while one was open for 3% of the time, Pallas kernels for 0%

profile of v1, /device:TPU:10, one launch (start us, length us, event | category | flops | bytes accessed | tf_op | source)
XLA Modules:
  0.0 120.0 jit_solution(3228166128050574945)
XLA Ops:
  0.6 1.3 %multiply_reduce_fusion = f32[2,2,160]{2,1,0:T(2,128)S(1)} fusion(bf16[2,2,160,384]{3,2,1,0:T(8,128)(2,1)} %param.7), kind=kLoop, calls=%fused_computation.66 | loop fusion | flops 736640 | bytes 494080 | tf_op jit(solution)/shard_map/reduce_sum | solution.py:49
  2.0 1.2 %multiply_convert_fusion.1 = bf16[2,2,160,384]{3,2,1,0:T(8,128)(2,1)S(1)} fusion(bf16[2,2,160,384]{3,2,1,0:T(8,128)(2,1)} %param.7, f32[384]{0:T(512)} %param.9, f32[2,2,160]{2,1,0:T(2,128)S(1)} %add_rsqrt_fusion.1), kind=kLoop, calls=%fused_computation.65 | loop fusion | flops 983040 | bytes 987136 | tf_op jit(solution)/shard_map/convert_element_type | solution.py:56
  3.2 1.7 %convolution_convert_fusion = bf16[640,768]{1,0:T(8,128)(2,1)S(1)} fusion(bf16[640,384]{1,0:T(8,128)(2,1)S(1)} %bitcast.152, bf16[384,1152]{1,0:T(8,128)(2,1)} %param.10), kind=kOutput, calls=%fused_computation.18 | convolution fusion | flops 377978880 | bytes 2064384 | tf_op jit(solution)/shard_map/dot_general | solution.py:66
  4.9 1.6 %collective-permute-start = (bf16[2,320,768]{2,1,0:T(8,128)(2,1)S(1)}, bf16[2,320,768]{2,1,0:T(8,128)(2,1)S(1)}, u32[]{:S(2)}, u32[]{:S(2)}) collective-permute-start(bf16[2,320,768]{2,1,0:T(8,128)(2,1)S(1)} %bitcast.180), channel_id=1, source_target_pairs={{0,4},{4,8},{8,12},{12,0},{1,5},{5,9},{9,13},{13,1},{2,6},{6,10},{... | collective-permute-start | bytes 2949128 | tf_op jit(solution)/shard_map/ppermute | solution.py:17
  7.0 22.6 %collective-permute-done = bf16[2,320,768]{2,1,0:T(8,128)(2,1)S(1)} collective-permute-done((bf16[2,320,768]{2,1,0:T(8,128)(2,1)S(1)}, bf16[2,320,768]{2,1,0:T(8,128)(2,1)S(1)}, u32[]{:S(2)}, u32[]{:S(2)}) %collective-permute-start) | collective-permute-done | bytes 983072 | tf_op jit(solution)/shard_map/ppermute | solution.py:17
  29.6 20.4 %collective-permute-start.2 = (bf16[2,320,768]{2,1,0:T(8,128)(2,1)S(1)}, bf16[2,320,768]{2,1,0:T(8,128)(2,1)}, u32[]{:S(2)}, u32[]{:S(2)}) collective-permute-start(bf16[2,320,768]{2,1,0:T(8,128)(2,1)S(1)} %collective-permute-done), channel_id=1, source_target_pairs={{0,4},{4,8},{8,12},{12,0},{1,5},{5,9},{9,13},{13,1},{2,6},{6,10},{... | collective-permute-start | bytes 2949128 | tf_op jit(solution)/shard_map/ppermute | solution.py:17
  50.4 1.4 %convolution_convert_fusion.1 = bf16[640,384]{1,0:T(8,128)(2,1)S(1)} fusion(bf16[640,384]{1,0:T(8,128)(2,1)S(1)} %bitcast.153, bf16[384,1152]{1,0:T(8,128)(2,1)} %param.10), kind=kOutput, calls=%fused_computation.46 | convolution fusion | flops 188989440 | bytes 1277952 | tf_op jit(solution)/shard_map/dot_general | solution.py:60
  51.9 1.3 %constant_dynamic-update-slice_fusion.1 = bf16[2,1280,768]{2,1,0:T(8,128)(2,1)S(1)} fusion(bf16[2,1280,768]{2,1,0:T(8,128)(2,1)S(1)} %constant_dynamic-update-slice_fusion.2, bf16[2,320,768]{2,1,0:T(8,128)(2,1)} %collective-permute-done.1, s32[]{:T(128)S(6)} %select_n.118), kind=kLoop, calls=%fused_computation.166 | loop fusion | bytes 1966084 | tf_op jit(solution)/shard_map/dynamic_update_slice | solution.py:21
  53.2 17.6 %collective-permute-done.2 = bf16[2,320,768]{2,1,0:T(8,128)(2,1)} collective-permute-done((bf16[2,320,768]{2,1,0:T(8,128)(2,1)S(1)}, bf16[2,320,768]{2,1,0:T(8,128)(2,1)}, u32[]{:S(2)}, u32[]{:S(2)}) %collective-permute-start.2) | collective-permute-done | bytes 983072 | tf_op jit(solution)/shard_map/ppermute | solution.py:17
  70.8 1.3 %constant_dynamic-update-slice_fusion = bf16[2,1280,768]{2,1,0:T(8,128)(2,1)S(1)} fusion(bf16[2,1280,768]{2,1,0:T(8,128)(2,1)S(1)} %constant_dynamic-update-slice_fusion.1, bf16[2,320,768]{2,1,0:T(8,128)(2,1)} %collective-permute-done.2, s32[]{:T(128)S(6)} %select_n.120), kind=kLoop, calls=%fused_computation.165 | loop fusion | bytes 1966084 | tf_op jit(solution)/shard_map/dynamic_update_slice | solution.py:18
  72.0 1.2 fusion.98
  73.2 0.6 fusion.1
  73.9 1.1 divide_convert_fusion
  76.0 1.9 %collective-permute-start.3 = (bf16[2,2,160,384]{3,2,1,0:T(8,128)(2,1)S(1)}, bf16[2,2,160,384]{3,2,1,0:T(8,128)(2,1)S(1)}, u32[]{:S(2)}, u32[]{:S(2)}) collective-permute-start(bf16[2,2,160,384]{3,2,1,0:T(8,128)(2,1)S(1)} %multiply_convert_fusion), channel_id=1, source_target_pairs={{0,1},{1,2},{2,3},{4,5},{5,6},{6,7},{8,9},{9,10},{10,11},{12,13},{... | collective-permute-start | bytes 1474568 | tf_op jit(solution)/shard_map/ppermute | solution.py:30
  78.0 8.2 %collective-permute-done.3 = bf16[2,2,160,384]{3,2,1,0:T(8,128)(2,1)S(1)} collective-permute-done((bf16[2,2,160,384]{3,2,1,0:T(8,128)(2,1)S(1)}, bf16[2,2,160,384]{3,2,1,0:T(8,128)(2,1)S(1)}, u32[]{:S(2)}, u32[]{:S(2)}) %collective-permute-start.3) | collective-permute-done | bytes 491552 | tf_op jit(solution)/shard_map/ppermute | solution.py:30
  86.3 3.4 %collective-permute-start.4 = (bf16[4,1,160,384]{3,2,1,0:T(8,128)(2,1)S(1)}, bf16[4,1,160,384]{3,2,1,0:T(8,128)(2,1)S(1)}, u32[]{:S(2)}, u32[]{:S(2)}) collective-permute-start(bf16[4,1,160,384]{3,2,1,0:T(8,128)(2,1)S(1)} %get-tuple-element.34), channel_id=1, source_target_pairs={{0,4},{4,8},{8,12},{1,5},{5,9},{9,13},{2,6},{6,10},{10,14},{3,7},{... | collective-permute-start | bytes 1474568 | tf_op jit(solution)/shard_map/ppermute | solution.py:40
  89.8 2.4 %collective-permute-start.5 = (bf16[4,1,160,384]{3,2,1,0:T(8,128)(2,1)S(1)}, bf16[4,1,160,384]{3,2,1,0:T(8,128)(2,1)S(1)}, u32[]{:S(2)}, u32[]{:S(2)}) collective-permute-start(bf16[4,1,160,384]{3,2,1,0:T(8,128)(2,1)S(1)} %get-tuple-element.35), channel_id=1, source_target_pairs={{4,0},{8,4},{12,8},{5,1},{9,5},{13,9},{6,2},{10,6},{14,10},{7,3},{... | collective-permute-start | bytes 1474568 | tf_op jit(solution)/shard_map/ppermute | solution.py:41
  92.7 4.3 %collective-permute-done.4 = bf16[4,1,160,384]{3,2,1,0:T(8,128)(2,1)S(1)} collective-permute-done((bf16[4,1,160,384]{3,2,1,0:T(8,128)(2,1)S(1)}, bf16[4,1,160,384]{3,2,1,0:T(8,128)(2,1)S(1)}, u32[]{:S(2)}, u32[]{:S(2)}) %collective-permute-start.4) | collective-permute-done | bytes 491552 | tf_op jit(solution)/shard_map/ppermute | solution.py:40
  97.0 3.4 %collective-permute-done.5 = bf16[4,1,160,384]{3,2,1,0:T(8,128)(2,1)S(1)} collective-permute-done((bf16[4,1,160,384]{3,2,1,0:T(8,128)(2,1)S(1)}, bf16[4,1,160,384]{3,2,1,0:T(8,128)(2,1)S(1)}, u32[]{:S(2)}, u32[]{:S(2)}) %collective-permute-start.5) | collective-permute-done | bytes 491552 | tf_op jit(solution)/shard_map/ppermute | solution.py:41
  100.5 1.2 select_maximum_fusion
  101.7 1.4 %slice_select_fusion = (bf16[2,2,160,384]{3,2,1,0:T(8,128)(2,1)S(1)}, bf16[2,2,160,384]{3,2,1,0:T(8,128)(2,1)S(1)}, bf16[2,2,160,384]{3,2,1,0:T(8,128)(2,1)S(1)}...) fusion(bf16[4,4,162,384]{3,2,1,0:T(8,128)(2,1)S(1)} %select_max, ...), kind=kLoop, calls=%fused_computation.71 | loop fusion | flops 2949120 | bytes 11796484 | tf_op jit(solution)/shard_map/jit(_where)/select_n | solution.py:109
  103.4 1.6 %slice_select_fusion.6 = (bf16[2,2,160,384]{3,2,1,0:T(8,128)(2,1)S(1)}, bf16[2,2,160,384]{3,2,1,0:T(8,128)(2,1)S(1)}, bf16[2,2,160,384]{3,2,1,0:T(8,128)(2,1)S(1...) fusion(bf16[4,3,160,384]{3,2,1,0:T(8,128)(2,1)S(1)} %get-tuple-, ...), kind=kLoop, calls=%fused_computation.77 | loop fusion | flops 3686400 | bytes 13762566 | tf_op jit(solution)/shard_map/jit(_where)/select_n | solution.py:109
  105.1 1.3 %slice-done.1 = s8[4194304]{0:T(1024)(128)(4,1)S(1)} async-done(((s8[7962624]{0:T(1024)(128)(4,1)}), s8[4194304]{0:T(1024)(128)(4,1)S(1)}, s32[]{:S(2)}) %slice-start.1) | async-done | bytes 4194328
  118.8 1.2 %fusion.13 = bf16[640,384]{1,0:T(8,128)(2,1)} fusion(f32[640,384]{1,0:T(8,128)S(1)} %convolution_add_fusion.1, bf16[640,384]{1,0:T(8,128)(2,1)S(1)} %bitcast.154, bf16[3,3,3,384,384]{4,3,2,1,0:T(8,128)(2,1)S(1)} %bitcast.149), kind=kOutput, calls=%fused_computation.48 | convolution fusion | flops 189235200 | bytes 2260992 | tf_op jit(solution)/shard_map/dot_general | solution.py:112
  (61 shorter events, 15.1 us)
Async XLA Ops:
  0.6 74.4 %copy-start = (bf16[384,384]{1,0:T(8,128)(2,1)S(1)}, bf16[384,384]{1,0:T(8,128)(2,1)}, u32[]{:S(2)}) copy-start(bf16[384,384]{1,0:T(8,128)(2,1)} %param.11) | copy-start | bytes 884740
  4.9 24.7 %collective-permute-start = (bf16[2,320,768]{2,1,0:T(8,128)(2,1)S(1)}, bf16[2,320,768]{2,1,0:T(8,128)(2,1)S(1)}, u32[]{:S(2)}, u32[]{:S(2)}) collective-permute-start(bf16[2,320,768]{2,1,0:T(8,128)(2,1)S(1)} %bitcast.180), channel_id=1, source_target_pairs={{0,4},{4,8},{8,12},{12,0},{1,5},{5,9},{9,13},{13,1},{2,6},{6,10},{... | collective-permute-start | bytes 2949128 | tf_op jit(solution)/shard_map/ppermute | solution.py:17
  6.6 45.3 %collective-permute-start.1 = (bf16[2,320,768]{2,1,0:T(8,128)(2,1)S(1)}, bf16[2,320,768]{2,1,0:T(8,128)(2,1)}, u32[]{:S(2)}, u32[]{:S(2)}) collective-permute-start(bf16[2,320,768]{2,1,0:T(8,128)(2,1)S(1)} %bitcast.181), channel_id=1, source_target_pairs={{0,12},{4,0},{8,4},{12,8},{1,13},{5,1},{9,5},{13,9},{2,14},{6,2},{... | collective-permute-start | bytes 2949128 | tf_op jit(solution)/shard_map/ppermute | solution.py:20
  29.6 41.1 %collective-permute-start.2 = (bf16[2,320,768]{2,1,0:T(8,128)(2,1)S(1)}, bf16[2,320,768]{2,1,0:T(8,128)(2,1)}, u32[]{:S(2)}, u32[]{:S(2)}) collective-permute-start(bf16[2,320,768]{2,1,0:T(8,128)(2,1)S(1)} %collective-permute-done), channel_id=1, source_target_pairs={{0,4},{4,8},{8,12},{12,0},{1,5},{5,9},{9,13},{13,1},{2,6},{6,10},{... | collective-permute-start | bytes 2949128 | tf_op jit(solution)/shard_map/ppermute | solution.py:17
  73.9 1.1 copy-start.2
  73.9 1.8 %copy-start.4 = (f32[384]{0:T(512)S(1)}, f32[384]{0:T(512)}, u32[]{:S(2)}) copy-start(f32[384]{0:T(512)} %param.12) | copy-start | bytes 4612
  75.0 17.2 %copy-start.5 = (s32[4]{0:T(128)S(1)}, s32[4]{0:T(128)}, u32[]{:S(2)}) copy-start(s32[4]{0:T(128)} %param.8) | copy-start | bytes 52
  75.6 41.1 %copy-start.3 = (bf16[640,384]{1,0:T(8,128)(2,1)}, bf16[640,384]{1,0:T(8,128)(2,1)S(1)}, u32[]{:S(2)}) copy-start(bf16[640,384]{1,0:T(8,128)(2,1)S(1)} %get-tuple-element.55) | copy-start | bytes 1474564
  76.0 10.1 %collective-permute-start.3 = (bf16[2,2,160,384]{3,2,1,0:T(8,128)(2,1)S(1)}, bf16[2,2,160,384]{3,2,1,0:T(8,128)(2,1)S(1)}, u32[]{:S(2)}, u32[]{:S(2)}) collective-permute-start(bf16[2,2,160,384]{3,2,1,0:T(8,128)(2,1)S(1)} %multiply_convert_fusion), channel_id=1, source_target_pairs={{0,1},{1,2},{2,3},{4,5},{5,6},{6,7},{8,9},{9,10},{10,11},{12,13},{... | collective-permute-start | bytes 1474568 | tf_op jit(solution)/shard_map/ppermute | solution.py:30
  86.3 10.7 %collective-permute-start.4 = (bf16[4,1,160,384]{3,2,1,0:T(8,128)(2,1)S(1)}, bf16[4,1,160,384]{3,2,1,0:T(8,128)(2,1)S(1)}, u32[]{:S(2)}, u32[]{:S(2)}) collective-permute-start(bf16[4,1,160,384]{3,2,1,0:T(8,128)(2,1)S(1)} %get-tuple-element.34), channel_id=1, source_target_pairs={{0,4},{4,8},{8,12},{1,5},{5,9},{9,13},{2,6},{6,10},{10,14},{3,7},{... | collective-permute-start | bytes 1474568 | tf_op jit(solution)/shard_map/ppermute | solution.py:40
  89.8 10.7 %collective-permute-start.5 = (bf16[4,1,160,384]{3,2,1,0:T(8,128)(2,1)S(1)}, bf16[4,1,160,384]{3,2,1,0:T(8,128)(2,1)S(1)}, u32[]{:S(2)}, u32[]{:S(2)}) collective-permute-start(bf16[4,1,160,384]{3,2,1,0:T(8,128)(2,1)S(1)} %get-tuple-element.35), channel_id=1, source_target_pairs={{4,0},{8,4},{12,8},{5,1},{9,5},{13,9},{6,2},{10,6},{14,10},{7,3},{... | collective-permute-start | bytes 1474568 | tf_op jit(solution)/shard_map/ppermute | solution.py:41
  103.1 2.1 %slice-start = ((s8[7962624]{0:T(1024)(128)(4,1)}), s8[3768320]{0:T(1024)(128)(4,1)S(1)}, s32[]{:S(2)}) async-start(s8[7962624]{0:T(1024)(128)(4,1)} %bitcast.148), calls=%async_computation | async-start | bytes 7536640
  103.4 3.1 %slice-start.1 = ((s8[7962624]{0:T(1024)(128)(4,1)}), s8[4194304]{0:T(1024)(128)(4,1)S(1)}, s32[]{:S(2)}) async-start(s8[7962624]{0:T(1024)(128)(4,1)} %bitcast.148), calls=%async_computation.1 | async-start | bytes 8388608
  117.4 2.7 %copy-start.1 = (bf16[384,384]{1,0:T(8,128)(2,1)S(1)}, bf16[384,384]{1,0:T(8,128)(2,1)}, u32[]{:S(2)}) copy-start(bf16[384,384]{1,0:T(8,128)(2,1)} %param.11) | copy-start | bytes 884740
